TPU v7x, 32 devices: a whole 2x2x4 slice. The times are simulated.
32 devices in a mesh: groups: 2 (over y), lat: 8 (over z, x), lon: 2 (over core).
Axes of the slice: x: 2, y: 2, z: 4, core: 2. Of those that a mesh axis runs over, the one named last changes fastest.
Arguments:
- tokens: bfloat16 [16, 256, 768], P(('groups', 'lat'), 'lon'), parts along dimension 0, may hold values from -5 to 5
- gain_attn: float32 [768], replicated, may hold values from 0.25 to 1.75
- w_qkv: bfloat16 [768, 2304], P('lat'), may hold values from -0.048353085 to 0.048353085
- key_bias: bfloat16 [8, 12, 256], P('lat', None, 'lon'), may hold values from -3 to 250
- w_out: bfloat16 [768, 768], P('lat'), may hold values from -0.21875 to 0.21875
- gain_conv: float32 [768], replicated, may hold values from 0.25 to 1.75
- w_conv: bfloat16 [2, 768, 64], replicated, may hold values from -0.75 to 0.75
- lat_taps: float32 [16, 2], replicated, may hold values from -2 to 2
- lon_half: int32 [8], P('lat'), may hold values from 1 to 128, as said below
- lat_half: int32 [8], P('lat'), may hold values from 0 to 1, as said below
- quad_off: int32 [8], P('lat'), may hold values from 0 to 13
Outputs:
- updated: bfloat16 [16, 256, 768], P(('groups', 'lat'), 'lon'), parts along dimension 0
There are 2 independent parts, one for each index of `groups`. A program takes and returns all parts, laid end to end along the dimension named above; an argument that names none is the same for every part. Nothing has to cross between parts.
Inputs may be any that keep to these rules, and one draw needn't show every extreme that they name: `lon_half`: the bands at either pole reach 128. `lat_half`: both polar bands have 1.
All inputs are finite; a program needn't handle non-finite values.
Results may differ from a plain program's by a relative error of at most 0.008.
Values may be sent and summed in bfloat16 or wider, within the bound.
A program may use at most 64 MiB of HBM per device.

v0:
```python
import jax
import jax.numpy as jnp
from jax import lax
from jax.sharding import PartitionSpec as P


def padded(cells, sides, width):
    for axis, dim in sides:
        count = lax.axis_size(axis)
        ends = count - 1
        head = lax.slice_in_dim(cells, 0, width, axis=dim)
        tail = lax.slice_in_dim(cells, cells.shape[dim] - width, cells.shape[dim], axis=dim)
        cells = jnp.concatenate(
            [
                lax.ppermute(tail, axis, [(i, (i + 1) % count) for i in range(ends)]),
                cells,
                lax.ppermute(head, axis, [((i + 1) % count, i) for i in range(ends)]),
            ],
            axis=dim,
        )
    return cells


def layer_norm(inputs, gain):
    values = inputs.astype(jnp.float32)
    average = jnp.mean(values, axis=-1, keepdims=True)
    centered = values - average
    variance = jnp.mean(centered * centered, axis=-1, keepdims=True)
    return centered * lax.rsqrt(variance + 1e-05) * gain


def group_mix(inputs, w_conv):
    basis, length, channels = inputs.shape
    group_width = w_conv.shape[2]
    groups = channels // group_width
    mixed_rows = jnp.einsum(
        "kjgc,kgce->kjge",
        inputs.reshape(basis, length, groups, group_width),
        w_conv.reshape(basis, groups, group_width, group_width),
        preferred_element_type=jnp.float32,
    )
    return mixed_rows.reshape(basis, length, channels).astype(jnp.bfloat16)


def lon_weights(row_ids, col_ids, half_width, lon_total):
    offset_lon = (
        jnp.mod(col_ids[None, :] - row_ids[:, None] + lon_total // 2, lon_total) - lon_total // 2
    )
    distance = jnp.abs(offset_lon).astype(jnp.float32)
    span_plus = (half_width + 1).astype(jnp.float32)
    tent_weight = jnp.where(
        distance <= half_width.astype(jnp.float32), (1.0 - distance / span_plus) / span_plus, 0.0
    )
    odd_weight = tent_weight * offset_lon.astype(jnp.float32) / span_plus
    return jnp.stack([tent_weight, odd_weight]).astype(jnp.bfloat16)


def start_state(query_count, head_count, head_dim):
    running_max = jnp.full((head_count, query_count), -jnp.inf, jnp.float32)
    running_sum = jnp.zeros((head_count, query_count), jnp.float32)
    running_out = jnp.zeros((query_count, head_count, head_dim), jnp.float32)
    return (running_max, running_sum, running_out)


def attend_keys(carry_state, queries, key_rows, value_rows, bias_rows, score_scale):
    key_count = key_rows.shape[0]
    for offset in range(0, key_count, 128):
        running_max, running_sum, running_out = carry_state
        key_block = key_rows[offset : offset + 128]
        value_block = value_rows[offset : offset + 128]
        bias_block = bias_rows[offset : offset + 128]
        scores = (
            jnp.einsum("qhd,khd->hqk", queries, key_block, preferred_element_type=jnp.float32)
            * score_scale
        )
        scores = scores + bias_block.T.astype(jnp.float32)[:, None, :]
        new_max = jnp.maximum(running_max, jnp.max(scores, axis=-1))
        rescale = jnp.exp(running_max - new_max)
        exp_scores = jnp.exp(scores - new_max[:, :, None])
        running_sum = running_sum * rescale + jnp.sum(exp_scores, axis=-1)
        running_out = running_out * rescale.T[:, :, None] + jnp.einsum(
            "hqk,khd->qhd",
            exp_scores.astype(jnp.bfloat16),
            value_block,
            preferred_element_type=jnp.float32,
        )
        carry_state = (new_max, running_sum, running_out)
    return carry_state


def finish_state(carry_state):
    running_max, running_sum, running_out = carry_state
    finished = running_out / running_sum.T[:, :, None]
    return finished.reshape(finished.shape[0], -1).astype(jnp.bfloat16)


def lon_conv(blended, half_width, first_col, out_cols):
    lon_total = blended.shape[1]
    block_cols = min(128, lon_total)
    block_count = lon_total // block_cols
    first_block = jnp.floor_divide(first_col - half_width, block_cols)
    last_block = jnp.floor_divide(first_col + out_cols - 1 + half_width, block_cols)
    turn_count = jnp.minimum(block_count, last_block - first_block + 1)
    row_ids = first_col + jnp.arange(out_cols, dtype=jnp.int32)

    def add_block(turn_index, running_out):
        block_at = jnp.mod(first_block + turn_index, block_count)
        lon_block = lax.dynamic_slice_in_dim(blended, block_at * block_cols, block_cols, 1)
        col_ids = block_at * block_cols + jnp.arange(block_cols, dtype=jnp.int32)
        coeffs = lon_weights(row_ids, col_ids, half_width, lon_total)
        return running_out + jnp.einsum(
            "kjc,kcd->jd", coeffs, lon_block, preferred_element_type=jnp.float32
        )

    initial = jnp.zeros((out_cols, blended.shape[2]), jnp.float32)
    return lax.fori_loop(0, turn_count, add_block, initial)


def per_device(
    tokens,
    gain_attn,
    w_qkv,
    key_bias,
    w_out,
    gain_conv,
    w_conv,
    lat_taps,
    lon_half,
    lat_half,
    quad_off,
):
    own_tokens = tokens[0]
    count_lon, model_width = own_tokens.shape
    head_count = key_bias.shape[1]
    head_dim = model_width // head_count
    score_scale = head_dim ** (-0.5)
    lon_place = lax.axis_index("lon")
    normed = layer_norm(own_tokens, gain_attn).astype(jnp.bfloat16)
    bias_rows = key_bias[0].T
    full_qkv, full_out = (
        lax.all_gather(w_qkv, "lat", axis=0, tiled=True),
        lax.all_gather(w_out, "lat", axis=0, tiled=True),
    )
    projected = jnp.dot(normed, full_qkv, preferred_element_type=jnp.float32).astype(jnp.bfloat16)
    queries = projected[:, :model_width].reshape(count_lon, head_count, head_dim)
    key_here = projected[:, model_width : 2 * model_width]
    value_here = projected[:, 2 * model_width :]
    key_piece = lax.all_gather(key_here, "lon", axis=0, tiled=True)
    value_piece = lax.all_gather(value_here, "lon", axis=0, tiled=True)
    bias_piece = lax.all_gather(bias_rows, "lon", axis=0, tiled=True)
    length = key_piece.shape[0]
    carry_state = attend_keys(
        start_state(count_lon, head_count, head_dim),
        queries,
        key_piece.reshape(length, head_count, head_dim),
        value_piece.reshape(length, head_count, head_dim),
        bias_piece,
        score_scale,
    )
    attended = finish_state(carry_state)
    branch_out = jnp.dot(attended, full_out, preferred_element_type=jnp.float32)
    middle = (own_tokens.astype(jnp.float32) + branch_out).astype(jnp.bfloat16)
    conv_in = layer_norm(middle, gain_conv).astype(jnp.bfloat16)
    stacked = padded(conv_in[None], (("lat", 0),), 1)
    lat_row = lax.axis_index("lat")
    last_band = lax.axis_size("lat") - 1
    offsets = jnp.arange(3, dtype=jnp.int32) - 1
    one_hot = (
        (quad_off[0] + offsets + 1)[:, None]
        == jnp.arange(lat_taps.shape[0], dtype=jnp.int32)[None, :]
    ).astype(jnp.float32)
    tap_vals = jnp.dot(one_hot, lat_taps, precision=lax.Precision.HIGHEST)
    tap_vals = jnp.where((jnp.abs(offsets) <= lat_half[0])[:, None], tap_vals, 0.0)
    summed = jnp.einsum(
        "rk,rjd->kjd", tap_vals, stacked.astype(jnp.float32), precision=lax.Precision.HIGHEST
    ).astype(jnp.bfloat16)
    pole_gain = jnp.where(lat_row == 0, tap_vals[0], 0.0) + jnp.where(
        lat_row == last_band, tap_vals[2], 0.0
    )
    first_col = lon_place * count_lon
    pole_rows = (pole_gain[:, None, None] * conv_in.astype(jnp.float32)[None]).astype(jnp.bfloat16)
    mixed_rows = group_mix(summed, w_conv)
    pole_mixed = group_mix(pole_rows, w_conv)
    circle_rows, pole_all = (
        lax.all_gather(mixed_rows, "lon", axis=1, tiled=True),
        lax.all_gather(pole_mixed, "lon", axis=1, tiled=True),
    )
    lon_total = circle_rows.shape[1]
    blended = (
        circle_rows.astype(jnp.float32)
        + jnp.roll(pole_all, -(lon_total // 2), axis=1).astype(jnp.float32)
    ).astype(jnp.bfloat16)
    conv_out = lon_conv(blended, lon_half[0], first_col, count_lon)
    return (middle.astype(jnp.float32) + conv_out).astype(jnp.bfloat16)[None]


def solution(mesh):
    return jax.shard_map(
        per_device,
        mesh=mesh,
        in_specs=(
            P(("groups", "lat"), "lon", None),
            P(),
            P("lat", None),
            P("lat", None, "lon"),
            P("lat", None),
            P(),
            P(),
            P(),
            P("lat"),
            P("lat"),
            P("lat"),
        ),
        out_specs=P(("groups", "lat"), "lon", None),
        check_vma=False,
    )
```

profile of v0, /device:TPU:9, one launch (start us, length us, event | category | flops | bytes accessed | tf_op | source)
XLA Modules:
  0.0 145.8 jit_solution(11945221781708907703)
XLA Ops:
  6.5 0.7 all-gather.3.cloned.1.call-update
  7.3 0.7 all-gather.5.cloned.1.call-update
  8.7 1.0 convert_reduce_fusion
  9.7 1.1 fusion.29
  10.9 2.5 %all_gather.23 = bf16[256,12]{0,1:T(8,128)(2,1)S(1)} all-gather(bf16[128,12]{0,1:T(8,128)(2,1)} %bitcast.119), channel_id=1, replica_groups=mesh['groups'=2,'lat'=8,'lon'=2] {'lon'}, dimensions={0}, use_global_device_ids=true | all-gather | bytes 9216 | tf_op jit(solution)/shard_map/all_gather | solution.py:150
  14.7 1.3 reshape.244
  16.4 58.0 %all-gather.3.cloned.1.call-done = bf16[768,2304]{1,0:T(8,128)(2,1)} async-done(((bf16[96,2304]{1,0:T(8,128)(2,1)}), bf16[768,2304]{1,0:T(8,128)(2,1)}) %all-gather.3.cloned.1.call-update) | async-done | bytes 3538960 | tf_op jit(solution)/shard_map/all_gather | solution.py:141
  74.4 2.7 %convolution_convert_fusion = bf16[128,2304]{1,0:T(8,128)(2,1)S(1)} fusion(bf16[768,2304]{1,0:T(8,128)(2,1)} %all-gather.3.cloned.1.call-done, bf16[1,128,768]{2,1,0:T(8,128)(2,1)S(1)} %copy-done.1, f32[768]{0:T(1024)S(1)} %copy-done.3, f32[128]{0:T(128)S(1)} %add_rsqrt_fusion.1, f32[128]{0:T(128)S(1)} %broadcast_multiply_fusion.1), kind=kOutput, calls=%fused_computation.20 | convolution fusion | flops 453771264 | bytes 4329472 | tf_op jit(solution)/shard_map/dot_general | solution.py:144
  77.1 3.7 %all_gather.22 = bf16[256,768]{1,0:T(8,128)(2,1)S(1)} all-gather(bf16[128,768]{1,0:T(8,128)(2,1)S(1)} %get-tuple-element.186), channel_id=1, replica_groups=mesh['groups'=2,'lat'=8,'lon'=2] {'lon'}, dimensions={0}, use_global_device_ids=true | all-gather | bytes 589824 | tf_op jit(solution)/shard_map/all_gather | solution.py:148
  81.3 2.1 %all_gather.24 = bf16[256,768]{1,0:T(8,128)(2,1)S(1)} all-gather(bf16[128,768]{1,0:T(8,128)(2,1)S(1)} %get-tuple-element.187), channel_id=1, replica_groups=mesh['groups'=2,'lat'=8,'lon'=2] {'lon'}, dimensions={0}, use_global_device_ids=true | all-gather | bytes 589824 | tf_op jit(solution)/shard_map/all_gather | solution.py:149
  83.8 0.4 fusion.58
  84.2 0.4 fusion.59
  84.7 0.3 fusion.22
  85.0 0.2 fusion.17
  85.2 0.2 fusion.18
  85.5 30.8 %all-gather.5.cloned.1.call-done = bf16[768,768]{1,0:T(8,128)(2,1)} async-done(((bf16[96,768]{1,0:T(8,128)(2,1)}), bf16[768,768]{1,0:T(8,128)(2,1)}) %all-gather.5.cloned.1.call-update) | async-done | bytes 1179664 | tf_op jit(solution)/shard_map/all_gather | solution.py:142
  116.3 1.7 %fusion.60 = (f32[128]{0:T(128)S(1)}, f32[128,768]{1,0:T(8,128)S(1)}) fusion(bf16[128,768]{0,1:T(8,128)(2,1)S(1)} %bitcast.117, bf16[768,768]{1,0:T(8,128)(2,1)} %all-gather.5.cloned.1.call-done, bf16[1,128,768]{2,1,0:T(8,128)(2,1)S(1)} %copy-done.1), kind=kOutput, calls=%fused_computation.99 | convolution fusion | flops 151486336 | bytes 1966592 | tf_op jit(solution)/shard_map/dot_general | solution.py:161
  118.0 0.2 multiply_reduce_fusion
  118.3 2.2 %collective-permute-start = (bf16[1,128,768]{2,1,0:T(8,128)(2,1)S(1)}, bf16[1,128,768]{2,1,0:T(8,128)(2,1)S(1)}, u32[]{:S(2)}, u32[]{:S(2)}) collective-permute-start(bf16[1,128,768]{2,1,0:T(8,128)(2,1)S(1)} %get-tuple-element.190), channel_id=1, source_target_pairs={{0,2},{2,4},{4,6},{6,8},{8,10},{10,12},{12,14},{1,3},{3,5},{5,7},{... | collective-permute-start | bytes 589832 | tf_op jit(solution)/shard_map/ppermute | solution.py:15
  120.5 4.0 %collective-permute-start.1 = (bf16[1,128,768]{2,1,0:T(8,128)(2,1)S(1)}, bf16[1,128,768]{2,1,0:T(8,128)(2,1)S(1)}, u32[]{:S(2)}, u32[]{:S(2)}) collective-permute-start(bf16[1,128,768]{2,1,0:T(8,128)(2,1)S(1)} %get-tuple-element.190), channel_id=1, source_target_pairs={{2,0},{4,2},{6,4},{8,6},{10,8},{12,10},{14,12},{3,1},{5,3},{7,5},{... | collective-permute-start | bytes 589832 | tf_op jit(solution)/shard_map/ppermute | solution.py:17
  124.7 0.3 convolution_convert_fusion.2
  125.2 4.1 %all_gather.27 = bf16[2,256,768]{2,1,0:T(8,128)(2,1)S(1)} all-gather(bf16[2,128,768]{2,1,0:T(8,128)(2,1)S(1)} %copy.40), channel_id=1, replica_groups=mesh['groups'=2,'lat'=8,'lon'=2] {'lon'}, dimensions={1}, use_global_device_ids=true | all-gather | bytes 1179648 | tf_op jit(solution)/shard_map/all_gather | solution.py:186
  129.4 2.8 %collective-permute-done.1 = bf16[1,128,768]{2,1,0:T(8,128)(2,1)S(1)} collective-permute-done((bf16[1,128,768]{2,1,0:T(8,128)(2,1)S(1)}, bf16[1,128,768]{2,1,0:T(8,128)(2,1)S(1)}, u32[]{:S(2)}, u32[]{:S(2)}) %collective-permute-start.1) | collective-permute-done | bytes 196640 | tf_op jit(solution)/shard_map/ppermute | solution.py:17
  132.2 1.4 convolution_convert_fusion.1
  133.7 0.5 copy.35
  134.2 0.3 convolution_convert_fusion.3
  134.6 2.5 %all_gather.26 = bf16[2,256,768]{2,1,0:T(8,128)(2,1)S(1)} all-gather(bf16[2,128,768]{2,1,0:T(8,128)(2,1)S(1)} %copy.37), channel_id=1, replica_groups=mesh['groups'=2,'lat'=8,'lon'=2] {'lon'}, dimensions={1}, use_global_device_ids=true | all-gather | bytes 1179648 | tf_op jit(solution)/shard_map/all_gather | solution.py:185
  137.1 0.2 add_convert_fusion
  137.4 0.9 while.14
  137.6 0.2 fusion.79
  138.0 0.2 fusion.79
  138.3 0.7 fusion.40
  (41 shorter events, 2.5 us)
Async XLA Ops:
  6.5 9.5 %copy-start = (f32[16,2]{0,1:T(2,128)S(1)}, f32[16,2]{0,1:T(2,128)}, u32[]{:S(2)}) copy-start(f32[16,2]{0,1:T(2,128)} %param.20) | copy-start | bytes 388
  6.5 67.8 %copy-start.1 = (bf16[1,128,768]{2,1,0:T(8,128)(2,1)S(1)}, bf16[1,128,768]{2,1,0:T(8,128)(2,1)}, u32[]{:S(2)}) copy-start(bf16[1,128,768]{2,1,0:T(8,128)(2,1)} %param.13) | copy-start | bytes 589828
  6.5 67.8 %copy-start.3 = (f32[768]{0:T(1024)S(1)}, f32[768]{0:T(1024)}, u32[]{:S(2)}) copy-start(f32[768]{0:T(1024)} %param.14) | copy-start | bytes 9220
  6.5 67.8 %all-gather.3.cloned.1.call-start = ((), (), s32[]{:S(2)}) async-start(), calls=%async_computation | async-start | bytes 3981312 | tf_op jit(solution)/shard_map/all_gather | solution.py:141
  7.3 109.0 %all-gather.5.cloned.1.call-start = ((), (), s32[]{:S(2)}) async-start(), calls=%async_computation.1 | async-start | bytes 1327104 | tf_op jit(solution)/shard_map/all_gather | solution.py:142
  85.5 32.7 %copy-start.2 = (f32[768]{0:T(1024)S(1)}, f32[768]{0:T(1024)}, u32[]{:S(2)}) copy-start(f32[768]{0:T(1024)} %param.18) | copy-start | bytes 9220
  118.3 11.1 %collective-permute-start = (bf16[1,128,768]{2,1,0:T(8,128)(2,1)S(1)}, bf16[1,128,768]{2,1,0:T(8,128)(2,1)S(1)}, u32[]{:S(2)}, u32[]{:S(2)}) collective-permute-start(bf16[1,128,768]{2,1,0:T(8,128)(2,1)S(1)} %get-tuple-element.190), channel_id=1, source_target_pairs={{0,2},{2,4},{4,6},{6,8},{8,10},{10,12},{12,14},{1,3},{3,5},{5,7},{... | collective-permute-start | bytes 589832 | tf_op jit(solution)/shard_map/ppermute | solution.py:15
  120.5 11.6 %collective-permute-start.1 = (bf16[1,128,768]{2,1,0:T(8,128)(2,1)S(1)}, bf16[1,128,768]{2,1,0:T(8,128)(2,1)S(1)}, u32[]{:S(2)}, u32[]{:S(2)}) collective-permute-start(bf16[1,128,768]{2,1,0:T(8,128)(2,1)S(1)} %get-tuple-element.190), channel_id=1, source_target_pairs={{2,0},{4,2},{6,4},{8,6},{10,8},{12,10},{14,12},{3,1},{5,3},{7,5},{... | collective-permute-start | bytes 589832 | tf_op jit(solution)/shard_map/ppermute | solution.py:17
Sparse Core Ops, SparseCore 0:
  9.5 64.7 all-gather.2
  76.6 39.6 all-gather.4
where the time goes:
time: 146 us
  waiting for transfers between devices  92.9 us (64%)
  between operations  15.7 us (11%)
  blocking collectives  14.8 us (10%)
  matrix products  8.42 us (6%)
  starting transfers between devices  6.22 us (4%)
  other arithmetic  4.29 us (3%)
  local copies, waits for them, and re-layouts  3.28 us (2%)
    all_gather x1, waiting for transfers between devices, per_device(): lax.all_gather(w_qkv, 'lat', axis=0, tiled=True)  58 us
    all_gather x1, waiting for transfers between devices, per_device(): lax.all_gather(w_out, 'lat', axis=0, tiled=True)  30.8 us
    all_gather x1, blocking collectives, per_device(): lax.all_gather(pole_mixed, 'lon', axis=1, tiled=True)  4.1 us
    ppermute x1, starting transfers between devices, padded(): lax.ppermute(head, axis, [((i + 1) % count, i) for i in range(ends)])  4 us
    all_gather x1, blocking collectives, per_device(): key_piece = lax.all_gather(key_here, 'lon', axis=0, tiled=True)  3.68 us
  transfers between devices with their start and end apart: 4, of which 3 were waited for; matrix products, arithmetic and copies ran while one was open for 7% of the time, Pallas kernels for 0%

commit v1 on v0

--- a/solution.py
+++ b/solution.py
@@ -2,6 +2,28 @@
 import jax.numpy as jnp
 from jax import lax
 from jax.sharding import PartitionSpec as P
+
+
+def laid_out(tiles, dim):
+    shape = list(tiles.shape[1:])
+    shape[dim] *= tiles.shape[0]
+    return jnp.moveaxis(tiles, 0, dim).reshape(shape)
+
+
+def collect(value, axis, dim):
+    size = lax.axis_size(axis)
+    pairs = [(i, (i + 1) % size) for i in range(size)]
+    back = [(b, a) for a, b in pairs]
+    lower, upper = ([], [])
+    for step in range(size - 1):
+        if step % 2 == 0:
+            lower.append(lax.ppermute(lower[-1] if lower else value, axis, pairs))
+        else:
+            upper.append(lax.ppermute(upper[-1] if upper else value, axis, back))
+    pieces = jnp.stack([*lower[::-1], value, *upper])
+    shift = lax.axis_index(axis) - len(lower)
+    pieces = pieces[(jnp.arange(size) - shift) % size]
+    return laid_out(pieces, dim)
 
 
 def padded(cells, sides, width):
@@ -139,7 +161,7 @@
     bias_rows = key_bias[0].T
     full_qkv, full_out = (
         lax.all_gather(w_qkv, "lat", axis=0, tiled=True),
-        lax.all_gather(w_out, "lat", axis=0, tiled=True),
+        collect(w_out, "lat", 0),
     )
     projected = jnp.dot(normed, full_qkv, preferred_element_type=jnp.float32).astype(jnp.bfloat16)
     queries = projected[:, :model_width].reshape(count_lon, head_count, head_dim)

time: 146 us -> 119 us (0.82)
  waiting for transfers between devices: 92.9 us -> 59.6 us
  starting transfers between devices: 6.22 us -> 13.8 us
    all_gather x1 -> x0, waiting for transfers between devices: 30.8 us -> none  [per_device(): lax.all_gather(w_out, 'lat', axis=0, tiled=True)]
    all_gather x1, waiting for transfers between devices: 58 us -> 37.6 us  [per_device(): lax.all_gather(w_qkv, 'lat', axis=0, tiled=True)]
    ppermute x0 -> x7, waiting for transfers between devices: none -> 17.4 us  [the longest x4 14.9 us: collect(): lower.append(lax.ppermute(lower[-1] if lower else value, axis, pairs))]
    ppermute x0 -> x7, starting transfers between devices: none -> 7.61 us  [the longest x3 4.6 us: collect(): upper.append(lax.ppermute(upper[-1] if upper else value, axis, back))]
  transfers between devices with their start and end apart: 4 -> 10, of which waited for: 3 -> 6; matrix products, arithmetic and copies ran while one was open for 7% -> 4% of each run, Pallas kernels for 0% -> 0%
where the time goes in v1:
time: 119 us
  waiting for transfers between devices  59.6 us (50%)
  between operations  15.8 us (13%)
  blocking collectives  14.2 us (12%)
  starting transfers between devices  13.8 us (12%)
  matrix products  7.15 us (6%)
  other arithmetic  4.34 us (4%)
  local copies, waits for them, and re-layouts  4.02 us (3%)
    all_gather x1, waiting for transfers between devices, per_device(): lax.all_gather(w_qkv, 'lat', axis=0, tiled=True)  37.6 us
    ppermute x4, waiting for transfers between devices, collect(): lower.append(lax.ppermute(lower[-1] if lower else value, axis, pairs))  14.9 us
    ppermute x3, starting transfers between devices, collect(): upper.append(lax.ppermute(upper[-1] if upper else value, axis, back))  4.6 us
    ppermute x1, waiting for transfers between devices, padded(): lax.ppermute(head, axis, [((i + 1) % count, i) for i in range(ends)])  3.93 us
    all_gather x1, blocking collectives, per_device(): key_piece = lax.all_gather(key_here, 'lon', axis=0, tiled=True)  3.68 us
    ppermute x1, starting transfers between devices, padded(): lax.ppermute(head, axis, [((i + 1) % count, i) for i in range(ends)])  3.14 us
    ppermute x1, starting transfers between devices, padded(): lax.ppermute(tail, axis, [(i, (i + 1) % count) for i in range(ends)])  3.04 us
    all_gather x1, blocking collectives, per_device(): bias_piece = lax.all_gather(bias_rows, 'lon', axis=0, tiled=True)  3.02 us
  transfers between devices with their start and end apart: 10, of which 6 were waited for; matrix products, arithmetic and copies ran while one was open for 4% of the time, Pallas kernels for 0%

profile of v1, /device:TPU:9, one launch (start us, length us, event | category | flops | bytes accessed | tf_op | source)
XLA Modules:
  0.0 119.1 jit_solution(9071557607907208161)
XLA Ops:
  6.5 0.7 all-gather.2.cloned.1.call-update
  7.3 1.3 %collective-permute-start = (bf16[96,768]{1,0:T(8,128)(2,1)}, bf16[96,768]{1,0:T(8,128)(2,1)S(1)}, u32[]{:S(2)}, u32[]{:S(2)}) collective-permute-start(bf16[96,768]{1,0:T(8,128)(2,1)} %param.17), channel_id=1, source_target_pairs={{0,2},{2,4},{4,6},{6,8},{8,10},{10,12},{12,14},{14,0},{1,3},{3,5},... | collective-permute-start | bytes 442376 | tf_op jit(solution)/shard_map/ppermute | solution.py:20
  8.5 1.2 collective-permute-start.4
  11.0 3.0 %all_gather.20 = bf16[256,12]{0,1:T(8,128)(2,1)S(1)} all-gather(bf16[128,12]{0,1:T(8,128)(2,1)} %bitcast.139), channel_id=1, replica_groups=mesh['groups'=2,'lat'=8,'lon'=2] {'lon'}, dimensions={0}, use_global_device_ids=true | all-gather | bytes 9216 | tf_op jit(solution)/shard_map/all_gather | solution.py:172
  14.2 1.1 convert_reduce_fusion
  15.3 0.4 collective-permute-start.1
  15.7 1.1 fusion.29
  16.8 4.2 %collective-permute-done.1 = bf16[96,768]{1,0:T(8,128)(2,1)S(1)} collective-permute-done((bf16[96,768]{1,0:T(8,128)(2,1)S(1)}, bf16[96,768]{1,0:T(8,128)(2,1)S(1)}, u32[]{:S(2)}, u32[]{:S(2)}) %collective-permute-start.1) | collective-permute-done | bytes 147488 | tf_op jit(solution)/shard_map/ppermute | solution.py:20
  21.0 2.4 %collective-permute-start.5 = (bf16[96,768]{1,0:T(8,128)(2,1)S(1)}, bf16[96,768]{1,0:T(8,128)(2,1)S(1)}, u32[]{:S(2)}, u32[]{:S(2)}) collective-permute-start(bf16[96,768]{1,0:T(8,128)(2,1)S(1)} %collective-permute-done.4), channel_id=1, source_target_pairs={{2,0},{4,2},{6,4},{8,6},{10,8},{12,10},{14,12},{0,14},{3,1},{5,3},... | collective-permute-start | bytes 442376 | tf_op jit(solution)/shard_map/ppermute | solution.py:22
  23.4 6.6 %collective-permute-done.2 = bf16[96,768]{1,0:T(8,128)(2,1)S(1)} collective-permute-done((bf16[96,768]{1,0:T(8,128)(2,1)S(1)}, bf16[96,768]{1,0:T(8,128)(2,1)S(1)}, u32[]{:S(2)}, u32[]{:S(2)}) %collective-permute-start.2) | collective-permute-done | bytes 147488 | tf_op jit(solution)/shard_map/ppermute | solution.py:20
  30.0 1.4 %collective-permute-start.3 = (bf16[96,768]{1,0:T(8,128)(2,1)S(1)}, bf16[96,768]{1,0:T(8,128)(2,1)S(1)}, u32[]{:S(2)}, u32[]{:S(2)}) collective-permute-start(bf16[96,768]{1,0:T(8,128)(2,1)S(1)} %collective-permute-done.2), channel_id=1, source_target_pairs={{0,2},{2,4},{4,6},{6,8},{8,10},{10,12},{12,14},{14,0},{1,3},{3,5},... | collective-permute-start | bytes 442376 | tf_op jit(solution)/shard_map/ppermute | solution.py:20
  32.0 1.3 %reshape.297 = bf16[2,12,64,64]{2,1,3,0:T(8,128)(2,1)S(1)} reshape(bf16[2,768,64]{1,2,0:T(8,128)(2,1)} %param.19) | data formatting | bytes 393216 | tf_op jit(solution)/shard_map/reshape | solution.py:61
  33.6 1.0 collective-permute-start.6
  34.6 4.2 %collective-permute-done.3 = bf16[96,768]{1,0:T(8,128)(2,1)S(1)} collective-permute-done((bf16[96,768]{1,0:T(8,128)(2,1)S(1)}, bf16[96,768]{1,0:T(8,128)(2,1)S(1)}, u32[]{:S(2)}, u32[]{:S(2)}) %collective-permute-start.3) | collective-permute-done | bytes 147488 | tf_op jit(solution)/shard_map/ppermute | solution.py:20
  38.9 2.5 %collective-permute-done.6 = bf16[96,768]{1,0:T(8,128)(2,1)S(1)} collective-permute-done((bf16[96,768]{1,0:T(8,128)(2,1)S(1)}, bf16[96,768]{1,0:T(8,128)(2,1)S(1)}, u32[]{:S(2)}, u32[]{:S(2)}) %collective-permute-start.6) | collective-permute-done | bytes 147488 | tf_op jit(solution)/shard_map/ppermute | solution.py:22
  41.4 0.6 gather_fusion
  42.1 37.6 %all-gather.2.cloned.1.call-done = bf16[768,2304]{1,0:T(8,128)(2,1)} async-done(((bf16[96,2304]{1,0:T(8,128)(2,1)}), bf16[768,2304]{1,0:T(8,128)(2,1)}) %all-gather.2.cloned.1.call-update) | async-done | bytes 3538960 | tf_op jit(solution)/shard_map/all_gather | solution.py:163
  79.7 2.7 %convolution_convert_fusion = bf16[128,2304]{1,0:T(8,128)(2,1)S(1)} fusion(bf16[768,2304]{1,0:T(8,128)(2,1)} %all-gather.2.cloned.1.call-done, bf16[1,128,768]{2,1,0:T(8,128)(2,1)S(1)} %copy-done.1, f32[768]{0:T(1024)S(1)} %copy-done.4, f32[128]{0:T(128)S(1)} %add_rsqrt_fusion.1, f32[128]{0:T(128)S(1)} %broadcast_multiply_fusion.1), kind=kOutput, calls=%fused_computation.21 | convolution fusion | flops 453771264 | bytes 4329472 | tf_op jit(solution)/shard_map/dot_general | solution.py:166
  82.4 3.7 %all_gather.19 = bf16[256,768]{1,0:T(8,128)(2,1)S(1)} all-gather(bf16[128,768]{1,0:T(8,128)(2,1)S(1)} %get-tuple-element.186), channel_id=1, replica_groups=mesh['groups'=2,'lat'=8,'lon'=2] {'lon'}, dimensions={0}, use_global_device_ids=true | all-gather | bytes 589824 | tf_op jit(solution)/shard_map/all_gather | solution.py:170
  86.6 2.1 %all_gather.21 = bf16[256,768]{1,0:T(8,128)(2,1)S(1)} all-gather(bf16[128,768]{1,0:T(8,128)(2,1)S(1)} %get-tuple-element.187), channel_id=1, replica_groups=mesh['groups'=2,'lat'=8,'lon'=2] {'lon'}, dimensions={0}, use_global_device_ids=true | all-gather | bytes 589824 | tf_op jit(solution)/shard_map/all_gather | solution.py:171
  89.1 0.4 fusion.60
  89.5 0.4 fusion.61
  90.8 0.4 fusion.62
  91.6 3.0 %collective-permute-start.7 = (bf16[1,128,768]{2,1,0:T(8,128)(2,1)S(1)}, bf16[1,128,768]{2,1,0:T(8,128)(2,1)S(1)}, u32[]{:S(2)}, u32[]{:S(2)}) collective-permute-start(bf16[1,128,768]{2,1,0:T(8,128)(2,1)S(1)} %get-tuple-element.190), channel_id=1, source_target_pairs={{0,2},{2,4},{4,6},{6,8},{8,10},{10,12},{12,14},{1,3},{3,5},{5,7},{... | collective-permute-start | bytes 589832 | tf_op jit(solution)/shard_map/ppermute | solution.py:37
  94.6 3.1 %collective-permute-start.8 = (bf16[1,128,768]{2,1,0:T(8,128)(2,1)S(1)}, bf16[1,128,768]{2,1,0:T(8,128)(2,1)S(1)}, u32[]{:S(2)}, u32[]{:S(2)}) collective-permute-start(bf16[1,128,768]{2,1,0:T(8,128)(2,1)S(1)} %get-tuple-element.190), channel_id=1, source_target_pairs={{2,0},{4,2},{6,4},{8,6},{10,8},{12,10},{14,12},{3,1},{5,3},{7,5},{... | collective-permute-start | bytes 589832 | tf_op jit(solution)/shard_map/ppermute | solution.py:39
  98.5 2.9 %all_gather.23 = bf16[2,256,768]{2,1,0:T(8,128)(2,1)S(1)} all-gather(bf16[2,128,768]{2,1,0:T(8,128)(2,1)S(1)} %copy.40), channel_id=1, replica_groups=mesh['groups'=2,'lat'=8,'lon'=2] {'lon'}, dimensions={1}, use_global_device_ids=true | all-gather | bytes 1179648 | tf_op jit(solution)/shard_map/all_gather | solution.py:208
  101.5 3.9 %collective-permute-done.8 = bf16[1,128,768]{2,1,0:T(8,128)(2,1)S(1)} collective-permute-done((bf16[1,128,768]{2,1,0:T(8,128)(2,1)S(1)}, bf16[1,128,768]{2,1,0:T(8,128)(2,1)S(1)}, u32[]{:S(2)}, u32[]{:S(2)}) %collective-permute-start.8) | collective-permute-done | bytes 196640 | tf_op jit(solution)/shard_map/ppermute | solution.py:39
  105.5 1.4 %convolution_convert_fusion.1 = bf16[2,128,768]{2,0,1:T(2,128)(2,1)S(1)} fusion(bf16[3,128,768]{2,1,0:T(8,128)(2,1)S(1)} %pad_maximum_fusion, f32[3,2]{0,1:T(2,128)S(1)} %convolution_select_fusion), kind=kOutput, calls=%fused_computation.27 | convolution fusion | flops 7274496 | bytes 983064 | tf_op jit(solution)/shard_map/rk,rjd->kjd/dot_general | solution.py:196
  106.9 0.5 copy.35
  107.9 2.5 %all_gather.22 = bf16[2,256,768]{2,1,0:T(8,128)(2,1)S(1)} all-gather(bf16[2,128,768]{2,1,0:T(8,128)(2,1)S(1)} %copy.37), channel_id=1, replica_groups=mesh['groups'=2,'lat'=8,'lon'=2] {'lon'}, dimensions={1}, use_global_device_ids=true | all-gather | bytes 1179648 | tf_op jit(solution)/shard_map/all_gather | solution.py:207
  110.6 0.9 while.14
  111.5 0.7 fusion.40
  (65 shorter events, 4.8 us)
Async XLA Ops:
  6.5 7.5 %copy-start = (f32[16,2]{0,1:T(2,128)S(1)}, f32[16,2]{0,1:T(2,128)}, u32[]{:S(2)}) copy-start(f32[16,2]{0,1:T(2,128)} %param.20) | copy-start | bytes 388
  6.5 73.1 %all-gather.2.cloned.1.call-start = ((), (), s32[]{:S(2)}) async-start(), calls=%async_computation | async-start | bytes 3981312 | tf_op jit(solution)/shard_map/all_gather | solution.py:163
  7.3 8.0 %collective-permute-start = (bf16[96,768]{1,0:T(8,128)(2,1)}, bf16[96,768]{1,0:T(8,128)(2,1)S(1)}, u32[]{:S(2)}, u32[]{:S(2)}) collective-permute-start(bf16[96,768]{1,0:T(8,128)(2,1)} %param.17), channel_id=1, source_target_pairs={{0,2},{2,4},{4,6},{6,8},{8,10},{10,12},{12,14},{14,0},{1,3},{3,5},... | collective-permute-start | bytes 442376 | tf_op jit(solution)/shard_map/ppermute | solution.py:20
  8.5 12.5 %collective-permute-start.4 = (bf16[96,768]{1,0:T(8,128)(2,1)}, bf16[96,768]{1,0:T(8,128)(2,1)S(1)}, u32[]{:S(2)}, u32[]{:S(2)}) collective-permute-start(bf16[96,768]{1,0:T(8,128)(2,1)} %param.17), channel_id=1, source_target_pairs={{2,0},{4,2},{6,4},{8,6},{10,8},{12,10},{14,12},{0,14},{3,1},{5,3},... | collective-permute-start | bytes 442376 | tf_op jit(solution)/shard_map/ppermute | solution.py:22
  14.2 24.7 %copy-start.2 = (bf16[96,768]{1,0:T(8,128)(2,1)S(1)}, bf16[96,768]{1,0:T(8,128)(2,1)}, u32[]{:S(2)}) copy-start(bf16[96,768]{1,0:T(8,128)(2,1)} %param.17) | copy-start | bytes 442372
  15.3 5.6 %collective-permute-start.1 = (bf16[96,768]{1,0:T(8,128)(2,1)S(1)}, bf16[96,768]{1,0:T(8,128)(2,1)S(1)}, u32[]{:S(2)}, u32[]{:S(2)}) collective-permute-start(bf16[96,768]{1,0:T(8,128)(2,1)S(1)} %collective-permute-done), channel_id=1, source_target_pairs={{0,2},{2,4},{4,6},{6,8},{8,10},{10,12},{12,14},{14,0},{1,3},{3,5},... | collective-permute-start | bytes 442376 | tf_op jit(solution)/shard_map/ppermute | solution.py:20
  21.0 9.0 %collective-permute-start.2 = (bf16[96,768]{1,0:T(8,128)(2,1)S(1)}, bf16[96,768]{1,0:T(8,128)(2,1)S(1)}, u32[]{:S(2)}, u32[]{:S(2)}) collective-permute-start(bf16[96,768]{1,0:T(8,128)(2,1)S(1)} %collective-permute-done.1), channel_id=1, source_target_pairs={{0,2},{2,4},{4,6},{6,8},{8,10},{10,12},{12,14},{14,0},{1,3},{3,5},... | collective-permute-start | bytes 442376 | tf_op jit(solution)/shard_map/ppermute | solution.py:20
  21.0 12.6 %collective-permute-start.5 = (bf16[96,768]{1,0:T(8,128)(2,1)S(1)}, bf16[96,768]{1,0:T(8,128)(2,1)S(1)}, u32[]{:S(2)}, u32[]{:S(2)}) collective-permute-start(bf16[96,768]{1,0:T(8,128)(2,1)S(1)} %collective-permute-done.4), channel_id=1, source_target_pairs={{2,0},{4,2},{6,4},{8,6},{10,8},{12,10},{14,12},{0,14},{3,1},{5,3},... | collective-permute-start | bytes 442376 | tf_op jit(solution)/shard_map/ppermute | solution.py:22
  30.0 8.8 %collective-permute-start.3 = (bf16[96,768]{1,0:T(8,128)(2,1)S(1)}, bf16[96,768]{1,0:T(8,128)(2,1)S(1)}, u32[]{:S(2)}, u32[]{:S(2)}) collective-permute-start(bf16[96,768]{1,0:T(8,128)(2,1)S(1)} %collective-permute-done.2), channel_id=1, source_target_pairs={{0,2},{2,4},{4,6},{6,8},{8,10},{10,12},{12,14},{14,0},{1,3},{3,5},... | collective-permute-start | bytes 442376 | tf_op jit(solution)/shard_map/ppermute | solution.py:20
  33.6 7.8 %collective-permute-start.6 = (bf16[96,768]{1,0:T(8,128)(2,1)S(1)}, bf16[96,768]{1,0:T(8,128)(2,1)S(1)}, u32[]{:S(2)}, u32[]{:S(2)}) collective-permute-start(bf16[96,768]{1,0:T(8,128)(2,1)S(1)} %collective-permute-done.5), channel_id=1, source_target_pairs={{2,0},{4,2},{6,4},{8,6},{10,8},{12,10},{14,12},{0,14},{3,1},{5,3},... | collective-permute-start | bytes 442376 | tf_op jit(solution)/shard_map/ppermute | solution.py:22
  41.4 38.2 %copy-start.1 = (bf16[1,128,768]{2,1,0:T(8,128)(2,1)S(1)}, bf16[1,128,768]{2,1,0:T(8,128)(2,1)}, u32[]{:S(2)}) copy-start(bf16[1,128,768]{2,1,0:T(8,128)(2,1)} %param.13) | copy-start | bytes 589828
  41.4 38.2 %copy-start.4 = (f32[768]{0:T(1024)S(1)}, f32[768]{0:T(1024)}, u32[]{:S(2)}) copy-start(f32[768]{0:T(1024)} %param.14) | copy-start | bytes 9220
  90.8 0.7 copy-start.3
  91.6 9.9 %collective-permute-start.7 = (bf16[1,128,768]{2,1,0:T(8,128)(2,1)S(1)}, bf16[1,128,768]{2,1,0:T(8,128)(2,1)S(1)}, u32[]{:S(2)}, u32[]{:S(2)}) collective-permute-start(bf16[1,128,768]{2,1,0:T(8,128)(2,1)S(1)} %get-tuple-element.190), channel_id=1, source_target_pairs={{0,2},{2,4},{4,6},{6,8},{8,10},{10,12},{12,14},{1,3},{3,5},{5,7},{... | collective-permute-start | bytes 589832 | tf_op jit(solution)/shard_map/ppermute | solution.py:37
  94.6 10.8 %collective-permute-start.8 = (bf16[1,128,768]{2,1,0:T(8,128)(2,1)S(1)}, bf16[1,128,768]{2,1,0:T(8,128)(2,1)S(1)}, u32[]{:S(2)}, u32[]{:S(2)}) collective-permute-start(bf16[1,128,768]{2,1,0:T(8,128)(2,1)S(1)} %get-tuple-element.190), channel_id=1, source_target_pairs={{2,0},{4,2},{6,4},{8,6},{10,8},{12,10},{14,12},{3,1},{5,3},{7,5},{... | collective-permute-start | bytes 589832 | tf_op jit(solution)/shard_map/ppermute | solution.py:39
Sparse Core Ops, SparseCore 0:
  9.5 70.0 all-gather.1
